TPU v7x, 512 devices: a whole 4x8x8 slice. The times are simulated.
512 devices in a mesh: ep: 128 (over z, y, core), tp: 4 (over x).
Axes of the slice: x: 4, y: 8, z: 8, core: 2. Of those that a mesh axis runs over, the one named last changes fastest.
Arguments:
- grad_out: bfloat16 [16384, 3584], P('ep', 'tp'), may hold values from -6 to 6
- routes: int32 [16384, 8], P('ep'), may hold values from 0 to 127, all different within a row; in each aligned block of 128 rows (0 to 127, 128 to 255, ...) at most 10 rows name the same one
- gate_weights: float32 [16384, 8], P('ep'), may hold values from 0.05 to 0.5
- gate_act: bfloat16 [128, 1280, 1024], P('ep', None, 'tp'), may hold values from -6 to 6
- w_down: bfloat16 [128, 1024, 3584], P('ep', None, 'tp'), may hold values from -0.1875 to 0.1875
- w_up: bfloat16 [128, 3584, 1024], P('ep', 'tp'), may hold values from -0.09375 to 0.09375
Outputs:
- grad_in: bfloat16 [16384, 3584], P('ep', 'tp')
Inputs may be any that keep to these rules, and one draw needn't show every extreme that they name: `routes`: each row names 8 different experts; among the 128 rows of one device no expert is named more than 10 times, a bound that some block reaches.
All inputs are finite; a program needn't handle non-finite values.
Results may differ from a plain program's by a relative error of at most 0.02.
Values may be sent and summed in bfloat16 or wider, within the bound.
A program may use at most 64 MiB of HBM per device.

v0:
```python
import jax
import jax.numpy as jnp
from jax import lax
from jax.sharding import PartitionSpec as P


def on_device(grad_out, routes, gate_weights, gate_act, w_down, w_up):
    experts_n = lax.axis_size("ep")
    slot_n = gate_act.shape[1] // experts_n
    rows_n = experts_n * slot_n
    token_n, choose_n = routes.shape
    flat_ids = routes.reshape(-1)
    one_hot = (flat_ids[:, None] == jnp.arange(experts_n, dtype=jnp.int32)[None, :]).astype(
        jnp.int32
    )
    earlier = jnp.cumsum(one_hot, axis=0) - one_hot
    slot_rank = jnp.sum(earlier * one_hot, axis=1)
    position = flat_ids * slot_n + slot_rank
    token_ids = jnp.arange(token_n * choose_n, dtype=jnp.int32) // choose_n
    token_of = jnp.full((rows_n,), token_n, jnp.int32).at[position].set(token_ids)
    weight_of = jnp.zeros((rows_n,), jnp.float32).at[position].set(gate_weights.reshape(-1))
    down_local = w_down[0]
    up_local = w_up[0]
    feat_part = grad_out.shape[1]
    padded = jnp.concatenate([grad_out, jnp.zeros((1, feat_part), grad_out.dtype)], axis=0)
    placed = (padded[token_of].astype(jnp.float32) * weight_of[:, None]).astype(jnp.bfloat16)
    placed = placed.reshape(experts_n, slot_n, feat_part)
    partial_value = jnp.einsum(
        "nsd,fd->nsf",
        lax.all_to_all(placed, "ep", split_axis=0, concat_axis=0, tiled=True),
        down_local,
        preferred_element_type=jnp.float32,
    )
    partial_value = partial_value.reshape(rows_n, -1)
    hidden_grad = lax.psum_scatter(
        partial_value.astype(jnp.bfloat16), "tp", scatter_dimension=1, tiled=True
    ).astype(jnp.float32)
    up_grad = (hidden_grad * gate_act[0].astype(jnp.float32)).astype(jnp.bfloat16)
    row_grad = lax.dot_general(
        lax.all_gather(up_grad, "tp", axis=1, tiled=True),
        up_local,
        (((1,), (1,)), ((), ())),
        preferred_element_type=jnp.float32,
    )
    row_grad = row_grad.astype(jnp.bfloat16).reshape(experts_n, slot_n, -1)
    returned = lax.all_to_all(row_grad, "ep", split_axis=0, concat_axis=0, tiled=True)
    picked = returned.reshape(rows_n, -1)[position]
    summed = jnp.sum(picked.astype(jnp.float32).reshape(token_n, choose_n, -1), axis=1)
    return summed.astype(jnp.bfloat16)


def solution(mesh):
    placed = (
        P("ep", "tp"),
        P("ep", None),
        P("ep", None),
        P("ep", None, "tp"),
        P("ep", None, "tp"),
        P("ep", "tp", None),
    )
    return jax.shard_map(
        on_device, mesh=mesh, in_specs=placed, out_specs=P("ep", "tp"), check_vma=False
    )
```

profile of v0, /device:TPU:24, one launch (start us, length us, event | category | flops | bytes accessed | tf_op | source)
XLA Modules:
  0.0 371.5 jit_solution(9736080060847365617)
XLA Ops:
  6.5 0.8 broadcast_multiply_fusion
  7.4 0.8 copy.8
  8.2 0.1 eq.29
  8.3 0.1 eq.25
  8.4 0.1 copy.7
  8.5 0.1 mul.35
  8.6 0.1 copy.10
  8.7 0.8 copy.12
  9.5 0.1 reshape.105
  9.5 0.2 fusion.5
  9.8 0.1 copy.11
  10.0 0.4 fusion.4
  10.3 4.3 %scatter_custom_fusion = s32[1280]{0:T(1024)S(1)} fusion(s32[1024]{0:T(1024)S(1)} %bitcast.28, s32[1024]{0:T(1024)S(1)} %add_select_fusion, s32[]{:T(128)} %constant.29.clone.1), kind=kCustom, calls=%fused_computation.33 | custom fusion | bytes 5124 | tf_op jit(solution)/shard_map/scatter | solution.py:20
  14.7 4.3 %scatter_custom_fusion.1 = f32[1280]{0:T(1024)S(1)} fusion(s32[1024]{0:T(1024)S(1)} %bitcast.29, f32[1024]{0:T(1024)S(1)} %reshape.105, f32[]{:T(128)} %constant.38.clone.1), kind=kCustom, calls=%fused_computation.31 | custom fusion | bytes 5124 | tf_op jit(solution)/shard_map/scatter | solution.py:21
  19.0 0.1 mul.37
  19.2 5.0 %gather_fusion = bf16[1280,896]{1,0:T(8,128)(2,1)} fusion(bf16[129,896]{1,0:T(8,128)(2,1)S(1)} %concatenate.3, s32[2048]{0:T(1024)S(1)} %pad_clamp_fusion), kind=kCustom, calls=%fused_computation | custom fusion | bytes 4592640 | tf_op jit(solution)/shard_map/gather | solution.py:26
  24.2 5.6 %reshape.75 = f32[128,10,896]{2,1,0:T(8,128)} reshape(bf16[1280,896]{1,0:T(8,128)(2,1)} %gather_fusion) | data formatting | bytes 6881280 | tf_op jit(solution)/shard_map/convert_element_type | solution.py:26
  29.8 3.6 multiply_convert_fusion
  33.4 105.1 %all_to_all.10 = bf16[128,10,896]{2,1,0:T(8,128)(2,1)} all-to-all(bf16[128,10,896]{2,1,0:T(8,128)(2,1)S(1)} %multiply_convert_fusion), channel_id=1, replica_groups=mesh['ep'=128,'tp'=4] {'ep'}, dimensions={0} | all-to-all | bytes 4587520 | tf_op jit(solution)/shard_map/all_to_all | solution.py:30
  138.5 5.3 %dot_general.8 = bf16[1280,896]{1,0:T(8,128)(2,1)} reshape(bf16[128,10,896]{2,1,0:T(8,128)(2,1)} %all_to_all.10) | data formatting | bytes 4587520 | tf_op jit(solution)/shard_map/nsd,fd->nsf/dot_general | solution.py:28
  143.9 5.9 %convolution_convert_fusion = bf16[1280,1024]{1,0:T(8,128)(2,1)} fusion(bf16[1280,896]{1,0:T(8,128)(2,1)} %dot_general.8, bf16[1,1024,896]{2,1,0:T(8,128)(2,1)S(1)} %copy-done), kind=kOutput, calls=%fused_computation.5 | convolution fusion | flops 2350120960 | bytes 6750208 | tf_op jit(solution)/shard_map/nsd,fd->nsf/dot_general | solution.py:28
  149.8 0.0 all-gather.2.cloned.1.call-start
  149.9 37.8 %reduce-scatter.2.cloned.1.call-done = bf16[1280,256]{1,0:T(8,128)(2,1)} async-done(((bf16[1280,1024]{1,0:T(8,128)(2,1)}), bf16[1280,256]{1,0:T(8,128)(2,1)}) %reduce-scatter.2.cloned.1.call-update) | async-done | bytes 655376 | tf_op jit(solution)/shard_map/reduce_scatter | solution.py:35
  187.6 2.1 fusion.2
  189.8 44.1 %all-gather.2.cloned.1.call-done = bf16[1280,1024]{1,0:T(8,128)(2,1)} async-done(((bf16[1280,256]{1,0:T(8,128)(2,1)}), bf16[1280,1024]{1,0:T(8,128)(2,1)}) %all-gather.2.cloned.1.call-update) | async-done | bytes 2621456 | tf_op jit(solution)/shard_map/all_gather | solution.py:40
  233.9 6.7 %convolution_convert_fusion.1 = bf16[1280,896]{1,0:T(8,128)(2,1)} fusion(bf16[1280,1024]{1,0:T(8,128)(2,1)} %all-gather.2.cloned.1.call-done, bf16[1,896,1024]{2,1,0:T(8,128)(2,1)} %param.11), kind=kOutput, calls=%fused_computation.6 | convolution fusion | flops 2349957120 | bytes 6750208 | tf_op jit(solution)/shard_map/dot_general | solution.py:39
  240.5 5.2 %reshape.73 = bf16[128,10,896]{2,1,0:T(8,128)(2,1)} reshape(bf16[1280,896]{1,0:T(8,128)(2,1)} %convolution_convert_fusion.1) | data formatting | bytes 4587520 | tf_op jit(solution)/shard_map/reshape | solution.py:45
  245.7 14.5 %all-to-all-start.1 = ((bf16[128,10,896]{2,1,0:T(8,128)(2,1)}), bf16[128,10,896]{2,1,0:T(8,128)(2,1)}, u32[]{:S(2)}, u32[]{:S(2)}) async-start(bf16[128,10,896]{2,1,0:T(8,128)(2,1)} %reshape.73), calls=%async_computation.2 | async-start | bytes 7340032 | tf_op jit(solution)/shard_map/all_to_all | solution.py:46
  260.2 88.0 %all-to-all-done.1 = bf16[128,10,896]{2,1,0:T(8,128)(2,1)} async-done(((bf16[128,10,896]{2,1,0:T(8,128)(2,1)}), bf16[128,10,896]{2,1,0:T(8,128)(2,1)}, u32[]{:S(2)}, u32[]{:S(2)}) %all-to-all-start.1) | async-done | bytes 2293792 | tf_op jit(solution)/shard_map/all_to_all | solution.py:46
  348.3 5.3 %reshape.74 = bf16[1280,896]{1,0:T(8,128)(2,1)} reshape(bf16[128,10,896]{2,1,0:T(8,128)(2,1)} %all-to-all-done.1) | data formatting | bytes 4587520 | tf_op jit(solution)/shard_map/reshape | solution.py:47
  353.6 7.7 %gather_fusion.1 = bf16[1024,896]{1,0:T(8,128)(2,1)} fusion(bf16[1280,896]{1,0:T(8,128)(2,1)} %reshape.74, s32[1024]{0:T(1024)S(1)} %broadcast_clamp_fusion), kind=kCustom, calls=%fused_computation.1 | custom fusion | bytes 3674112 | tf_op jit(solution)/shard_map/gather | solution.py:47
  361.3 3.4 bitcast_reduce_fusion
  (19 shorter events, 0.2 us)
Async XLA Ops:
  6.5 137.3 %copy-start = (bf16[1,1024,896]{2,1,0:T(8,128)(2,1)S(1)}, bf16[1,1024,896]{2,1,0:T(8,128)(2,1)}, u32[]{:S(2)}) copy-start(bf16[1,1024,896]{2,1,0:T(8,128)(2,1)} %param.10) | copy-start | bytes 5505028
  6.5 12.6 %copy-start.2 = (bf16[128,896]{1,0:T(8,128)(2,1)S(1)}, bf16[128,896]{1,0:T(8,128)(2,1)}, u32[]{:S(2)}) copy-start(bf16[128,896]{1,0:T(8,128)(2,1)} %param.6) | copy-start | bytes 688132
  6.5 181.1 %reduce-scatter.2.cloned.1.call-start = ((), (), s32[]{:S(2)}) async-start(), calls=%async_computation.3 | async-start | bytes 3276800 | tf_op jit(solution)/shard_map/reduce_scatter | solution.py:35
  149.8 37.8 %copy-start.1 = (bf16[1,1280,256]{2,1,0:T(8,128)(2,1)S(1)}, bf16[1,1280,256]{2,1,0:T(8,128)(2,1)}, u32[]{:S(2)}) copy-start(bf16[1,1280,256]{2,1,0:T(8,128)(2,1)} %param.9) | copy-start | bytes 1966084
  149.8 84.0 %all-gather.2.cloned.1.call-start = ((), (), s32[]{:S(2)}) async-start(), calls=%async_computation.4 | async-start | bytes 3276800 | tf_op jit(solution)/shard_map/all_gather | solution.py:40
  245.7 102.6 %all-to-all-start.1 = ((bf16[128,10,896]{2,1,0:T(8,128)(2,1)}), bf16[128,10,896]{2,1,0:T(8,128)(2,1)}, u32[]{:S(2)}, u32[]{:S(2)}) async-start(bf16[128,10,896]{2,1,0:T(8,128)(2,1)} %reshape.73), calls=%async_computation.2 | async-start | bytes 7340032 | tf_op jit(solution)/shard_map/all_to_all | solution.py:46
Sparse Core Ops, SparseCore 0:
  149.9 37.6 reduce-scatter.1
  189.9 43.9 all-gather.1
where the time goes:
time: 372 us
  waiting for transfers between devices  170 us (46%)
  blocking collectives  105 us (28%)
  local copies, waits for them, and re-layouts  45.2 us (12%)
  starting transfers between devices  14.6 us (4%)
  between operations  13.5 us (4%)
  matrix products  12.6 us (3%)
  other arithmetic  10.6 us (3%)
    all_to_all x1, blocking collectives, on_device(): lax.all_to_all(placed, 'ep', split_axis=0, concat_axis=0, tiled=True)  105 us
    all_to_all x1, waiting for transfers between devices, on_device(): lax.all_to_all(row_grad, 'ep', split_axis=0, concat_axis=0, tiled=True)  88 us
    all_gather x1, waiting for transfers between devices, on_device(): lax.all_gather(up_grad, 'tp', axis=1, tiled=True)  44.1 us
    reduce_scatter x1, waiting for transfers between devices, on_device(): lax.psum_scatter(partial_value.astype(jnp.bfloat16), 'tp', scatter_dimens...  37.8 us
    all_to_all x1, starting transfers between devices, on_device(): lax.all_to_all(row_grad, 'ep', split_axis=0, concat_axis=0, tiled=True)  14.5 us
    gather x1, local copies, waits for them, and re-layouts, on_device(): picked = returned.reshape(rows_n, -1)[position]  7.67 us
  transfers between devices with their start and end apart: 3, of which 3 were waited for; matrix products, arithmetic and copies ran while one was open for 0% of the time, Pallas kernels for 0%

commit v1 on v0

--- a/solution.py
+++ b/solution.py
@@ -2,6 +2,16 @@
 import jax.numpy as jnp
 from jax import lax
 from jax.sharding import PartitionSpec as P
+
+
+def begin_cycles_up(body, lane_axis, join_dim):
+    lower = jnp.concatenate(
+        lax.all_to_all(
+            jnp.stack([body for _ in range(lax.psum(1, lane_axis))], 0), lane_axis, 0, 0
+        ),
+        join_dim,
+    )
+    return lower
 
 
 def on_device(grad_out, routes, gate_weights, gate_act, w_down, w_up):
@@ -37,7 +47,7 @@
     ).astype(jnp.float32)
     up_grad = (hidden_grad * gate_act[0].astype(jnp.float32)).astype(jnp.bfloat16)
     row_grad = lax.dot_general(
-        lax.all_gather(up_grad, "tp", axis=1, tiled=True),
+        begin_cycles_up(up_grad, "tp", 1),
         up_local,
         (((1,), (1,)), ((), ())),
         preferred_element_type=jnp.float32,

time: 372 us -> 360 us (0.968)
  waiting for transfers between devices: 170 us -> 126 us
  blocking collectives: 105 us -> 140 us
    all_gather x1 -> x0, waiting for transfers between devices: 44.1 us -> none  [on_device(): lax.all_gather(up_grad, 'tp', axis=1, tiled=True)]
    all_to_all x0 -> x1, blocking collectives: none -> 34.9 us  [begin_cycles_up(): lax.all_to_all(jnp.stack([body for _ in range(lax.psum(1, lane_axis))], 0...]
  transfers between devices with their start and end apart: 3 -> 2, of which waited for: 3 -> 2; matrix products, arithmetic and copies ran while one was open for 0% -> 0% of each run, Pallas kernels for 0% -> 0%
where the time goes in v1:
time: 360 us; the launch traced here: 359 us
  blocking collectives  140 us (39%)
  waiting for transfers between devices  126 us (35%)
  local copies, waits for them, and re-layouts  45.6 us (13%)
  starting transfers between devices  14.5 us (4%)
  between operations  13.5 us (4%)
  matrix products  10.2 us (3%)
  other arithmetic  9.74 us (3%)
    all_to_all x1, blocking collectives, on_device(): lax.all_to_all(placed, 'ep', split_axis=0, concat_axis=0, tiled=True)  105 us
    all_to_all x1, waiting for transfers between devices, on_device(): lax.all_to_all(row_grad, 'ep', split_axis=0, concat_axis=0, tiled=True)  88 us
    reduce_scatter x1, waiting for transfers between devices, on_device(): lax.psum_scatter(partial_value.astype(jnp.bfloat16), 'tp', scatter_dimens...  37.8 us
    all_to_all x1, blocking collectives, begin_cycles_up(): lax.all_to_all(jnp.stack([body for _ in range(lax.psum(1, lane_axis))], 0...  34.9 us
    all_to_all x1, starting transfers between devices, on_device(): lax.all_to_all(row_grad, 'ep', split_axis=0, concat_axis=0, tiled=True)  14.5 us
    gather x1, local copies, waits for them, and re-layouts, on_device(): picked = returned.reshape(rows_n, -1)[position]  7.67 us
  transfers between devices with their start and end apart: 2, of which 2 were waited for; matrix products, arithmetic and copies ran while one was open for 0% of the time, Pallas kernels for 0%

profile of v1, /device:TPU:24, one launch (start us, length us, event | category | flops | bytes accessed | tf_op | source)
XLA Modules:
  0.0 359.4 jit_solution(16583294730819005968)
XLA Ops:
  6.5 0.8 broadcast_multiply_fusion
  7.4 0.8 copy.8
  8.2 0.1 eq.29
  8.4 0.1 copy.7
  8.5 0.1 mul.35
  8.6 0.1 copy.10
  8.7 0.8 copy.12
  9.5 0.1 reshape.115
  9.5 0.2 fusion.5
  9.8 0.1 copy.11
  10.0 0.4 fusion.4
  10.3 4.3 %scatter_custom_fusion = s32[1280]{0:T(1024)S(1)} fusion(s32[1024]{0:T(1024)S(1)} %bitcast.32, s32[1024]{0:T(1024)S(1)} %add_select_fusion, s32[]{:T(128)} %constant.29.clone.1), kind=kCustom, calls=%fused_computation.33 | custom fusion | bytes 5124 | tf_op jit(solution)/shard_map/scatter | solution.py:30
  14.7 4.3 %scatter_custom_fusion.1 = f32[1280]{0:T(1024)S(1)} fusion(s32[1024]{0:T(1024)S(1)} %bitcast.33, f32[1024]{0:T(1024)S(1)} %reshape.115, f32[]{:T(128)} %constant.38.clone.1), kind=kCustom, calls=%fused_computation.31 | custom fusion | bytes 5124 | tf_op jit(solution)/shard_map/scatter | solution.py:31
  19.0 0.1 mul.37
  19.2 5.0 %gather_fusion = bf16[1280,896]{1,0:T(8,128)(2,1)} fusion(bf16[129,896]{1,0:T(8,128)(2,1)S(1)} %concatenate.3, s32[2048]{0:T(1024)S(1)} %pad_clamp_fusion), kind=kCustom, calls=%fused_computation | custom fusion | bytes 4592640 | tf_op jit(solution)/shard_map/gather | solution.py:36
  24.2 5.6 %reshape.85 = f32[128,10,896]{2,1,0:T(8,128)} reshape(bf16[1280,896]{1,0:T(8,128)(2,1)} %gather_fusion) | data formatting | bytes 6881280 | tf_op jit(solution)/shard_map/convert_element_type | solution.py:36
  29.8 3.6 multiply_convert_fusion
  33.4 105.1 %all_to_all.15 = bf16[128,10,896]{2,1,0:T(8,128)(2,1)} all-to-all(bf16[128,10,896]{2,1,0:T(8,128)(2,1)S(1)} %multiply_convert_fusion), channel_id=1, replica_groups=mesh['ep'=128,'tp'=4] {'ep'}, dimensions={0} | all-to-all | bytes 4587520 | tf_op jit(solution)/shard_map/all_to_all | solution.py:40
  138.5 5.3 %dot_general.8 = bf16[1280,896]{1,0:T(8,128)(2,1)} reshape(bf16[128,10,896]{2,1,0:T(8,128)(2,1)} %all_to_all.15) | data formatting | bytes 4587520 | tf_op jit(solution)/shard_map/nsd,fd->nsf/dot_general | solution.py:38
  143.9 5.9 %convolution_convert_fusion = bf16[1280,1024]{1,0:T(8,128)(2,1)} fusion(bf16[1280,896]{1,0:T(8,128)(2,1)} %dot_general.8, bf16[1,1024,896]{2,1,0:T(8,128)(2,1)S(1)} %copy-done), kind=kOutput, calls=%fused_computation.5 | convolution fusion | flops 2350120960 | bytes 6750208 | tf_op jit(solution)/shard_map/nsd,fd->nsf/dot_general | solution.py:38
  149.8 37.8 %reduce-scatter.2.cloned.1.call-done = bf16[1280,256]{1,0:T(8,128)(2,1)} async-done(((bf16[1280,1024]{1,0:T(8,128)(2,1)}), bf16[1280,256]{1,0:T(8,128)(2,1)}) %reduce-scatter.2.cloned.1.call-update) | async-done | bytes 655376 | tf_op jit(solution)/shard_map/reduce_scatter | solution.py:45
  187.6 1.3 fusion.2
  188.9 0.2 copy.13
  189.1 0.2 stack.2
  189.3 34.9 %all_to_all.16 = bf16[4,1280,256]{1,2,0:T(8,128)(2,1)S(1)} all-to-all(bf16[4,1280,256]{1,2,0:T(8,128)(2,1)S(1)} %stack.2), channel_id=1, replica_groups=mesh['ep'=128,'tp'=4] {'tp'}, dimensions={0} | all-to-all | bytes 5242880 | tf_op jit(solution)/shard_map/all_to_all | solution.py:9
  224.2 4.2 %convolution_convert_fusion.1 = bf16[1280,896]{1,0:T(8,128)(2,1)} fusion(bf16[1280,1024]{0,1:T(8,128)(2,1)S(1)} %bitcast.30, bf16[1,896,1024]{2,1,0:T(8,128)(2,1)S(1)} %copy-done.3), kind=kOutput, calls=%fused_computation.6 | convolution fusion | flops 2349957120 | bytes 6750208 | tf_op jit(solution)/shard_map/dot_general | solution.py:49
  228.4 5.2 %reshape.83 = bf16[128,10,896]{2,1,0:T(8,128)(2,1)} reshape(bf16[1280,896]{1,0:T(8,128)(2,1)} %convolution_convert_fusion.1) | data formatting | bytes 4587520 | tf_op jit(solution)/shard_map/reshape | solution.py:55
  233.6 14.5 %all-to-all-start.2 = ((bf16[128,10,896]{2,1,0:T(8,128)(2,1)}), bf16[128,10,896]{2,1,0:T(8,128)(2,1)}, u32[]{:S(2)}, u32[]{:S(2)}) async-start(bf16[128,10,896]{2,1,0:T(8,128)(2,1)} %reshape.83), calls=%async_computation.3 | async-start | bytes 7340032 | tf_op jit(solution)/shard_map/all_to_all | solution.py:56
  248.1 88.0 %all-to-all-done.2 = bf16[128,10,896]{2,1,0:T(8,128)(2,1)} async-done(((bf16[128,10,896]{2,1,0:T(8,128)(2,1)}), bf16[128,10,896]{2,1,0:T(8,128)(2,1)}, u32[]{:S(2)}, u32[]{:S(2)}) %all-to-all-start.2) | async-done | bytes 2293792 | tf_op jit(solution)/shard_map/all_to_all | solution.py:56
  336.2 5.3 %reshape.84 = bf16[1280,896]{1,0:T(8,128)(2,1)} reshape(bf16[128,10,896]{2,1,0:T(8,128)(2,1)} %all-to-all-done.2) | data formatting | bytes 4587520 | tf_op jit(solution)/shard_map/reshape | solution.py:57
  341.5 7.7 %gather_fusion.1 = bf16[1024,896]{1,0:T(8,128)(2,1)} fusion(bf16[1280,896]{1,0:T(8,128)(2,1)} %reshape.84, s32[1024]{0:T(1024)S(1)} %broadcast_clamp_fusion), kind=kCustom, calls=%fused_computation.1 | custom fusion | bytes 3674112 | tf_op jit(solution)/shard_map/gather | solution.py:57
  349.2 3.4 bitcast_reduce_fusion
  (21 shorter events, 0.2 us)
Async XLA Ops:
  6.5 137.3 %copy-start = (bf16[1,1024,896]{2,1,0:T(8,128)(2,1)S(1)}, bf16[1,1024,896]{2,1,0:T(8,128)(2,1)}, u32[]{:S(2)}) copy-start(bf16[1,1024,896]{2,1,0:T(8,128)(2,1)} %param.10) | copy-start | bytes 5505028
  6.5 12.6 %copy-start.2 = (bf16[128,896]{1,0:T(8,128)(2,1)S(1)}, bf16[128,896]{1,0:T(8,128)(2,1)}, u32[]{:S(2)}) copy-start(bf16[128,896]{1,0:T(8,128)(2,1)} %param.6) | copy-start | bytes 688132
  6.5 181.1 %reduce-scatter.2.cloned.1.call-start = ((), (), s32[]{:S(2)}) async-start(), calls=%async_computation.4 | async-start | bytes 3276800 | tf_op jit(solution)/shard_map/reduce_scatter | solution.py:45
  149.8 37.8 %copy-start.1 = (bf16[1,1280,256]{2,1,0:T(8,128)(2,1)S(1)}, bf16[1,1280,256]{2,1,0:T(8,128)(2,1)}, u32[]{:S(2)}) copy-start(bf16[1,1280,256]{2,1,0:T(8,128)(2,1)} %param.9) | copy-start | bytes 1966084
  189.3 34.9 %copy-start.3 = (bf16[1,896,1024]{2,1,0:T(8,128)(2,1)S(1)}, bf16[1,896,1024]{2,1,0:T(8,128)(2,1)}, u32[]{:S(2)}) copy-start(bf16[1,896,1024]{2,1,0:T(8,128)(2,1)} %param.11) | copy-start | bytes 5505028
  233.6 102.5 %all-to-all-start.2 = ((bf16[128,10,896]{2,1,0:T(8,128)(2,1)}), bf16[128,10,896]{2,1,0:T(8,128)(2,1)}, u32[]{:S(2)}, u32[]{:S(2)}) async-start(bf16[128,10,896]{2,1,0:T(8,128)(2,1)} %reshape.83), calls=%async_computation.3 | async-start | bytes 7340032 | tf_op jit(solution)/shard_map/all_to_all | solution.py:56
Sparse Core Ops, SparseCore 0:
  149.9 37.6 reduce-scatter.1
